TPU v7x, 128 devices: a whole 4x4x4 slice. The times are simulated.
128 devices in a mesh: row: 8 (over z_hi, y), col: 16 (over z_lo, x, core).
Axes of the slice: x: 4, y: 4, z: 4 (z_hi: 2, z_lo: 2; z = z_hi * 2 + z_lo), core: 2. Of those that a mesh axis runs over, the one named last changes fastest.
Arguments:
- features: float32 [2, 131072, 256], P(None, ('row', 'col')), may hold values from -7 to 7
- adj_vals: bfloat16 [2, 1024, 20, 128, 128], P(None, ('row', 'col')), may hold values from 0.049804688 to 1
- blk_cols: int32 [2, 1024, 20], P(None, ('row', 'col')), may hold values from 0 to 11
- blk_count: int32 [2, 1024], P(None, ('row', 'col')), may hold values from 1 to 20
- send_list: int32 [2, 128, 512], P(None, ('row', 'col')), may hold values from 0 to 1023
- weight: float32 [256, 256], replicated, may hold values from -0.375 to 0.375
- cand_tiles: int32 [8, 16, 2, 48], P('row', 'col'), may hold values from 0 to 127, as said below
- cand_count: int32 [8, 16], P('row', 'col'), may hold values from 8 to 48, as said below
Outputs:
- log_plan: float32 [8, 16, 48, 128, 128], P('row', 'col')
- row_potential: float32 [8, 16, 1024], P('row')
- col_potential: float32 [8, 16, 1024], P(None, 'col')
Inputs may be any that keep to these rules, and one draw needn't show every extreme that they name: Blocks at or past blk_count are padding. send_list[g, q, p * 4 + i] is the i-th own row that partition q sends to partition p. `cand_tiles`: every slot, live or not, holds a valid pair; no live pair repeats on one device; every tile of every source group and of every target group lies in some live slot; for each device and each partition of its row, at most 3 of the device's 48 slots name source tiles of that partition, and on every device some partition has exactly 3. `cand_count`: some device has all 48 slots live.
All inputs are finite; a program needn't handle non-finite values.
Results may differ from a plain program's by a relative error of at most 0.0003.
Values sent between devices are 32-bit elements; how exact they have to be, the bound alone decides.
A program may use at most 128 MiB of HBM per device.

v0:
```python
import math
import jax
import jax.numpy as jnp
from jax import lax
from jax.sharding import Mesh
from jax.sharding import PartitionSpec as P

TILE = 128
TD = 8
CAP = 48
ITERS = 2
COL = ("col_0", "col_1", "col_2")
ROW_COL = ("row", "col_0", "col_1", "col_2")
HIGHEST = lax.Precision.HIGHEST
SHARPNESS = 2.0
NEGATIVE = -1e30


def joined_all(array, axes, combine):
    for axis in axes:
        pieces = jax.tree.map(lambda part: lax.all_gather(part, axis), array)
        array = jax.tree.map(lambda part: part[0], pieces)
        for k in range(1, lax.axis_size(axis)):
            array = combine(array, jax.tree.map(lambda part: part[k], pieces))
    return array


def from_everyone(array, axis):
    size = lax.axis_size(axis)
    return lax.all_to_all(
        jnp.broadcast_to(array[None], (size, *array.shape)), axis, 0, 0, tiled=True
    )


def gathered_once(array, axis):
    leaves = jax.tree.leaves(array)
    turns = sorted(range(len(leaves)), key=lambda k: -leaves[k].size)
    width = (1, *leaves[turns[0]].shape)[-1]
    lines = [
        jnp.pad(leaves[k].reshape(-1), (0, -leaves[k].size % width)).reshape(-1, width)
        for k in turns
    ]
    both, at, found = (from_everyone(jnp.concatenate(lines), axis), 0, {})
    for k, line in zip(turns, lines):
        share = both[:, at : at + len(line)].reshape(len(both), -1)
        found[k] = share[:, : leaves[k].size].reshape(-1, *leaves[k].shape)
        at += len(line)
    numbers = iter(range(len(leaves)))
    return jax.tree.map(lambda _: found[next(numbers)], array)


def gathered_by_type(array, axis):
    leaves, found = (jax.tree.leaves(array), {})
    for leading, a in enumerate(leaves):
        if leading not in found:
            alike = [k for k, b in enumerate(leaves) if b.dtype == a.dtype]
            got = (
                gathered_once([leaves[k] for k in alike], axis)
                if len(alike) > 1
                else [from_everyone(a, axis)]
            )
            for k, b in zip(alike, got):
                found[k] = b
    numbers = iter(range(len(leaves)))
    return jax.tree.map(lambda _: found[next(numbers)], array)


def joined_by_halves(pieces, combine):
    while len(jax.tree.leaves(pieces)[0]) > 1:
        pieces = jax.vmap(combine)(
            *(jax.tree.map(lambda part: part[side::2], pieces) for side in (0, 1))
        )
    return jax.tree.map(lambda part: part[0], pieces)


def combined_all(array, axis, combine):
    pieces = gathered_by_type(array, axis)
    return joined_by_halves(pieces, combine)


def aggregate(lookup, block_vals, block_cols, block_count, weight, own_rows):
    num_tiles = block_vals.shape[0]
    listed = (jnp.arange(block_vals.shape[1])[None, :] < block_count[:, None]).astype(jnp.float32)

    def add_block(state_pair, block_index):
        summed, degree = state_pair
        weights_now = (
            block_vals[:, block_index].astype(jnp.float32) * listed[:, block_index][:, None, None]
        )
        picked = lookup[block_cols[:, block_index]]
        summed = summed + jnp.einsum("tij,tjd->tid", weights_now, picked, precision=HIGHEST)
        degree = degree + jnp.sum(weights_now, axis=2)
        return ((summed, degree), None)

    start_sum = jnp.zeros((num_tiles, TILE, lookup.shape[2]), jnp.float32)
    start_deg = jnp.zeros((num_tiles, TILE), jnp.float32)
    (summed, degree), unused = lax.scan(
        add_block, (start_sum, start_deg), jnp.arange(block_vals.shape[1])
    )
    mixed_rows = (summed / jnp.sqrt(degree)[:, :, None]).reshape(num_tiles * TILE, -1)
    return own_rows + jax.nn.relu(jnp.dot(mixed_rows, weight, precision=HIGHEST))


def pick_rows(source_rows, picked_rows):
    return source_rows[picked_rows]


def combine_lse(first_pair, second_pair):
    larger = jnp.maximum(first_pair[0], second_pair[0])
    merged_sum = first_pair[1] * jnp.exp(first_pair[0] - larger) + second_pair[1] * jnp.exp(
        second_pair[0] - larger
    )
    return (larger, merged_sum)


def lookup_rows(one_hot, table_values):
    return jnp.dot(one_hot, table_values, precision=HIGHEST)


def row_potential_of(values, grouped, picker, live_float):
    slot_max = jnp.max(values, axis=2)
    group_max = jnp.max(jnp.where(grouped[:, :, None], slot_max[:, None, :], NEGATIVE), axis=0)
    shift_back = lookup_rows(picker, group_max)
    slot_sums = jnp.sum(jnp.exp(values - shift_back[:, :, None]), axis=2)
    group_sum = jnp.einsum("sr,sc->rc", live_float, slot_sums, precision=HIGHEST)
    group_max, group_sum = joined_all((group_max, group_sum), COL, combine_lse)
    return -(group_max + jnp.log(group_sum))


def col_potential_of(values, grouped, picker, live_float):
    slot_max = jnp.max(values, axis=1)
    group_max = jnp.max(jnp.where(grouped[:, :, None], slot_max[:, None, :], NEGATIVE), axis=0)
    shift_back = lookup_rows(picker, group_max)
    slot_sums = jnp.sum(jnp.exp(values - shift_back[:, None, :]), axis=1)
    group_sum = jnp.einsum("sr,sc->rc", live_float, slot_sums, precision=HIGHEST)
    group_max, group_sum = combined_all((group_max, group_sum), "row", combine_lse)
    return -(group_max + jnp.log(group_sum))


def on_device(features, adj_vals, blk_cols, blk_count, send_list, weight, cand_tiles, cand_count):
    feat_width = features.shape[2]
    outgoing = jax.vmap(pick_rows)(features, send_list[:, 0])
    ghost_rows = lax.all_to_all(outgoing, ROW_COL, split_axis=1, concat_axis=1, tiled=True)
    embedded = []
    for graph_id in range(2):
        lookup = jnp.concatenate([features[graph_id], ghost_rows[graph_id]], axis=0).reshape(
            -1, TILE, feat_width
        )
        embedded.append(
            aggregate(
                lookup,
                adj_vals[graph_id],
                blk_cols[graph_id],
                blk_count[graph_id],
                weight,
                features[graph_id],
            )
        )
    source_embed = embedded[0]
    target_embed = embedded[1]
    row_count = lax.axis_size("row")
    col_count = lax.axis_size(COL)
    rows_here = cand_tiles[0, 0, 0]
    cols_here = cand_tiles[0, 0, 1]
    slot_index = jnp.arange(CAP, dtype=jnp.int32)
    slot_live = slot_index < cand_count[0, 0]
    target_group = lax.all_gather(target_embed, "row", axis=0, tiled=True).reshape(
        -1, TILE, feat_width
    )
    target_tiles = target_group[cols_here]
    source_group = lax.all_gather(source_embed, COL, axis=0, tiled=True).reshape(
        -1, TILE, feat_width
    )
    source_tiles = source_group[rows_here]
    logits = (
        SHARPNESS
        / math.sqrt(feat_width)
        * jnp.einsum("sid,sjd->sij", source_tiles, target_tiles, precision=HIGHEST)
    )
    row_onehot = rows_here[:, None] == jnp.arange(TD * col_count, dtype=jnp.int32)[None, :]
    col_onehot = cols_here[:, None] == jnp.arange(TD * row_count, dtype=jnp.int32)[None, :]
    row_grouped = row_onehot & slot_live[:, None]
    col_grouped = col_onehot & slot_live[:, None]
    row_picker = row_onehot.astype(jnp.float32)
    col_picker = col_onehot.astype(jnp.float32)
    row_livef = row_grouped.astype(jnp.float32)
    col_livef = col_grouped.astype(jnp.float32)
    live_cube = slot_live[:, None, None]
    col_pot = jnp.zeros((TD * row_count, TILE), jnp.float32)
    row_pot = jnp.zeros((TD * col_count, TILE), jnp.float32)
    for sweep_id in range(ITERS):
        col_slot = lookup_rows(col_picker, col_pot)
        values = jnp.where(live_cube, logits + col_slot[:, None, :], NEGATIVE)
        row_pot = row_potential_of(values, row_grouped, row_picker, row_livef)
        row_slot = lookup_rows(row_picker, row_pot)
        values = jnp.where(live_cube, logits + row_slot[:, :, None], NEGATIVE)
        col_pot = col_potential_of(values, col_grouped, col_picker, col_livef)
    row_slot = lookup_rows(row_picker, row_pot)
    col_slot = lookup_rows(col_picker, col_pot)
    log_plan = jnp.where(live_cube, logits + row_slot[:, :, None] + col_slot[:, None, :], 0.0)
    return (
        log_plan[None, None],
        row_pot.reshape(1, col_count, -1),
        col_pot.reshape(row_count, 1, -1),
    )


def solution(mesh):
    finer = Mesh(
        mesh.devices.reshape(mesh.shape["row"], 2, 4, 2), ("row", "col_0", "col_1", "col_2")
    )
    placed = (
        P(None, ROW_COL, None),
        P(None, ROW_COL, None, None, None),
        P(None, ROW_COL, None),
        P(None, ROW_COL),
        P(None, ROW_COL, None),
        P(),
        P("row", COL, None, None),
        P("row", COL),
    )
    return jax.shard_map(
        on_device,
        mesh=finer,
        in_specs=placed,
        out_specs=(P("row", COL, None, None, None), P("row", None, None), P(None, COL, None)),
        check_vma=False,
    )
```

profile of v0, /device:TPU:1, one launch (start us, length us, event | category | flops | bytes accessed | tf_op | source)
XLA Modules:
  0.0 697.5 jit_solution(7761243411783571190)
XLA Ops:
  7.9 12.6 %gather_fusion.4 = f32[1024,256]{1,0:T(8,128)S(1)} fusion(f32[2,1024,256]{2,1,0:T(8,128)} %param.12, s32[1024]{0:T(1024)S(1)} %bitcast.240), kind=kCustom, calls=%fused_computation.4 | custom fusion | bytes 2105344 | tf_op jit(solution)/shard_map/vmap()/gather | solution.py:105
  22.4 11.5 %all-to-all-start = ((f32[2,512,256]{2,0,1:T(2,128)}), f32[2,512,256]{2,0,1:T(2,128)S(1)}, u32[]{:S(2)}, u32[]{:S(2)}) async-start(f32[2,512,256]{2,0,1:T(2,128)} %copy.24), calls=%async_computation | async-start | bytes 2097152 | tf_op jit(solution)/shard_map/all_to_all | solution.py:143
  34.0 12.8 %fusion.125 = (bf16[1,8,20,128,128]{4,3,2,1,0:T(8,128)(2,1)}, bf16[1,8,20,128,128]{4,3,2,1,0:T(8,128)(2,1)}) fusion(bf16[2,8,20,128,128]{4,3,2,1,0:T(8,128)(2,1)} %param.13), kind=kLoop, calls=%fused_computation.219 | loop fusion | bytes 20971520 | tf_op jit(solution)/shard_map/slice | solution.py:152
  48.5 12.7 %copy_bitcast_fusion = (bf16[8,20,128,128]{3,2,0,1:T(8,128)(2,1)}, bf16[8,20,128,128]{3,2,0,1:T(8,128)(2,1)}) fusion(bf16[1,8,20,128,128]{4,3,2,1,0:T(8,128)(2,1)} %get-tuple-element.195, bf16[1,8,20,128,128]{4,3,2,1,0:T(8,128)(2,1)} %get-tuple-element.196), kind=kLoop, calls=%fused_computation.33 | loop fusion | bytes 20971520 | tf_op jit(solution)/shard_map/squeeze | solution.py:152
  64.3 180.3 %while.27 = (s32[]{:T(128)}, f32[8,128,256]{2,1,0:T(8,128)}, f32[8,128]{1,0:T(8,128)S(1)}, s32[20]{0:T(128)S(1)}, bf16[8,20,128,128]{3,2,0,1:T(8,128)(2,1)}, /*i...) while((s32[]{:T(128)}, f32[8,128,256]{2,1,0:T(8,128)}, ...), condition=%wide.region_5.6_spmd.clone, body=%wide.region_3.5_spmd.clone.sunk | while | flops 403834912 | bytes 5788086 | solution.py:97
  68.7 3.0 convolution_add_fusion.5
  77.3 3.4 convolution_add_fusion.5
  86.4 3.4 convolution_add_fusion.5
  95.4 3.4 convolution_add_fusion.5
  104.4 3.4 convolution_add_fusion.5
  113.5 3.4 convolution_add_fusion.5
  122.5 3.4 convolution_add_fusion.5
  131.5 3.4 convolution_add_fusion.5
  140.6 3.4 convolution_add_fusion.5
  149.6 3.4 convolution_add_fusion.5
  158.6 3.4 convolution_add_fusion.5
  167.7 3.4 convolution_add_fusion.5
  176.7 3.4 convolution_add_fusion.5
  185.7 3.4 convolution_add_fusion.5
  194.8 3.4 convolution_add_fusion.5
  203.8 3.4 convolution_add_fusion.5
  212.8 3.4 convolution_add_fusion.5
  221.9 3.4 convolution_add_fusion.5
  230.9 3.4 convolution_add_fusion.5
  239.9 3.4 convolution_add_fusion.5
  250.6 186.6 %while.26 = (s32[]{:T(128)}, f32[8,128,256]{2,1,0:T(8,128)}, f32[8,128]{1,0:T(8,128)S(1)}, s32[20]{0:T(128)S(1)}, bf16[8,20,128,128]{3,2,0,1:T(8,128)(2,1)}, /*i...) while((s32[]{:T(128)}, f32[8,128,256]{2,1,0:T(8,128)}, ...), condition=%wide.region_2.3_spmd.clone, body=%wide.region_0.2_spmd.clone.sunk | while | flops 403834912 | bytes 5788086 | solution.py:97
  255.3 3.1 convolution_add_fusion.4
  264.3 3.5 convolution_add_fusion.4
  273.6 3.5 convolution_add_fusion.4
  283.0 3.5 convolution_add_fusion.4
  292.3 3.7 convolution_add_fusion.4
  301.9 3.5 convolution_add_fusion.4
  311.2 3.5 convolution_add_fusion.4
  320.6 3.5 convolution_add_fusion.4
  329.9 3.5 convolution_add_fusion.4
  339.3 3.5 convolution_add_fusion.4
  348.6 3.5 convolution_add_fusion.4
  357.9 3.5 convolution_add_fusion.4
  367.3 3.5 convolution_add_fusion.4
  376.6 3.5 convolution_add_fusion.4
  385.9 3.5 convolution_add_fusion.4
  395.3 3.5 convolution_add_fusion.4
  404.6 3.5 convolution_add_fusion.4
  413.9 3.5 convolution_add_fusion.4
  423.2 3.5 convolution_add_fusion.4
  432.6 3.5 convolution_add_fusion.4
  441.8 7.0 %gather_fusion.3 = f32[48,128,256]{2,1,0:T(8,128)} fusion(f32[64,128,256]{2,1,0:T(8,128)} %bitcast.243, s32[1024]{0:T(1024)S(1)} %get-tuple-element.225), kind=kCustom, calls=%fused_computation.3 | custom fusion | bytes 12583104 | tf_op jit(solution)/shard_map/gather | solution.py:170
  448.9 85.5 %all-gather.7.cloned.1.call-done = f32[16384,256]{1,0:T(8,128)} async-done(((f32[1024,256]{1,0:T(8,128)}), f32[16384,256]{1,0:T(8,128)}) %all-gather.7.cloned.1.call-update) | async-done | bytes 16777232 | tf_op jit(solution)/shard_map/all_gather | solution.py:171
  534.4 9.4 %gather_fusion.2 = f32[48,128,256]{2,1,0:T(8,128)} fusion(f32[128,128,256]{2,1,0:T(8,128)} %bitcast.247, s32[1024]{0:T(1024)S(1)} %get-tuple-element.226), kind=kCustom, calls=%fused_computation.2 | custom fusion | bytes 12583104 | tf_op jit(solution)/shard_map/gather | solution.py:174
  543.7 9.2 %fusion.14 = (f32[48,128]{1,0:T(8,128)S(1)}, f32[48,128,128]{2,1,0:T(8,128)S(1)}) fusion(f32[48,128]{1,0:T(8,128)S(1)} %fusion.88, pred[48]{0:T(512)(128)(4,1)S(1)} %iota_compare_fusion.13, f32[48,128,256]{2,1,0:T(8,128)} %gather_fusion.2, f32[48,128,256]{2,1,0:T(8,128)} %gather_fusion.3), kind=kOutput, calls=%fused_computation.46 | convolution fusion | flops 2419058688 | bytes 15777840 | tf_op jit(solution)/shard_map/sid,sjd->sij/dot_general | solution.py:178
  554.4 3.8 all-gather
  560.6 3.8 all-gather.1
  564.5 9.4 %all_gather.66 = f32[4,128,128]{2,1,0:T(8,128)S(1)} all-gather(f32[1,128,128]{2,1,0:T(8,128)S(1)} %get-tuple-element.194), channel_id=1, replica_groups=mesh['row'=8,'col_0'=2,'col_1'=4,'col_2'=2] {'col_1'}, dimensions={0}, use_global_device_ids=true | all-gather | bytes 327680 | tf_op jit(solution)/shard_map/all_gather | solution.py:21
  573.8 10.2 %all_gather.70 = f32[4,128,128]{2,1,0:T(8,128)S(1)} all-gather(f32[1,128,128]{2,1,0:T(8,128)S(1)} %get-tuple-element.193), channel_id=1, replica_groups=mesh['row'=8,'col_0'=2,'col_1'=4,'col_2'=2] {'col_1'}, dimensions={0}, use_global_device_ids=true | all-gather | bytes 327680 | tf_op jit(solution)/shard_map/all_gather | solution.py:21
  584.2 9.4 %all_gather.67 = f32[2,128,128]{2,1,0:T(8,128)S(1)} all-gather(f32[1,128,128]{2,1,0:T(8,128)S(1)} %get-tuple-element.192), channel_id=1, replica_groups=mesh['row'=8,'col_0'=2,'col_1'=4,'col_2'=2] {'col_2'}, dimensions={0}, use_global_device_ids=true | all-gather | bytes 196608 | tf_op jit(solution)/shard_map/all_gather | solution.py:21
  599.2 17.5 %all_to_all.15 = f32[8,128,128]{2,1,0:T(8,128)S(1)} all-to-all(f32[8,128,128]{2,1,0:T(8,128)S(1)} %broadcast_in_dim.144), channel_id=1, replica_groups=mesh['row'=8,'col_0'=2,'col_1'=4,'col_2'=2] {'row'}, dimensions={0} | all-to-all | bytes 1048576 | tf_op jit(solution)/shard_map/all_to_all | solution.py:30
  619.7 3.8 all-gather.2
  626.0 3.8 all-gather.3
  629.8 9.4 %all_gather.74 = f32[4,128,128]{2,1,0:T(8,128)S(1)} all-gather(f32[1,128,128]{2,1,0:T(8,128)S(1)} %get-tuple-element.186), channel_id=1, replica_groups=mesh['row'=8,'col_0'=2,'col_1'=4,'col_2'=2] {'col_1'}, dimensions={0}, use_global_device_ids=true | all-gather | bytes 327680 | tf_op jit(solution)/shard_map/all_gather | solution.py:21
  639.2 9.4 %all_gather.78 = f32[4,128,128]{2,1,0:T(8,128)S(1)} all-gather(f32[1,128,128]{2,1,0:T(8,128)S(1)} %get-tuple-element.185), channel_id=1, replica_groups=mesh['row'=8,'col_0'=2,'col_1'=4,'col_2'=2] {'col_1'}, dimensions={0}, use_global_device_ids=true | all-gather | bytes 327680 | tf_op jit(solution)/shard_map/all_gather | solution.py:21
  649.2 10.8 %all_gather.75 = f32[2,128,128]{2,1,0:T(8,128)S(1)} all-gather(f32[1,128,128]{2,1,0:T(8,128)S(1)} %get-tuple-element.184), channel_id=1, replica_groups=mesh['row'=8,'col_0'=2,'col_1'=4,'col_2'=2] {'col_2'}, dimensions={0}, use_global_device_ids=true | all-gather | bytes 196608 | tf_op jit(solution)/shard_map/all_gather | solution.py:21
  670.3 4.2 all-to-all-start.2
  678.4 7.9 %all-to-all-done.2 = f32[8,128,128]{2,1,0:T(8,128)} async-done(((f32[8,128,128]{2,1,0:T(8,128)}), f32[8,128,128]{2,1,0:T(8,128)}, u32[]{:S(2)}, u32[]{:S(2)}) %all-to-all-start.2) | async-done | bytes 524320 | tf_op jit(solution)/shard_map/all_to_all | solution.py:30
  687.7 3.0 select_bitcast_fusion
  (388 shorter events, 203.3 us)
Async XLA Ops:
  7.2 238.9 %copy-start = (f32[256,256]{1,0:T(8,128)S(1)}, f32[256,256]{1,0:T(8,128)}, u32[]{:S(2)}) copy-start(f32[256,256]{1,0:T(8,128)} %param.17) | copy-start | bytes 786436
  22.4 38.9 %all-to-all-start = ((f32[2,512,256]{2,0,1:T(2,128)}), f32[2,512,256]{2,0,1:T(2,128)S(1)}, u32[]{:S(2)}, u32[]{:S(2)}) async-start(f32[2,512,256]{2,0,1:T(2,128)} %copy.24), calls=%async_computation | async-start | bytes 2097152 | tf_op jit(solution)/shard_map/all_to_all | solution.py:143
  33.9 408.0 %all-gather.9.cloned.1.call-start = ((), (), s32[]{:S(2)}) async-start(), calls=%async_computation.4 | async-start | bytes 9437184 | tf_op jit(solution)/shard_map/all_gather | solution.py:167
  34.0 12.9 %copy-start.11 = (s32[2,8]{1,0:T(2,128)S(1)}, s32[2,8]{1,0:T(2,128)}, u32[]{:S(2)}) copy-start(s32[2,8]{1,0:T(2,128)} %param.15) | copy-start | bytes 196
  34.0 12.9 %copy-start.7 = (s32[2,8,20]{2,1,0:T(8,128)S(1)}, s32[2,8,20]{2,1,0:T(8,128)}, u32[]{:S(2)}) copy-start(s32[2,8,20]{2,1,0:T(8,128)} %param.14) | copy-start | bytes 3844
  34.0 13.0 %copy-start.1 = (f32[2,1024,256]{2,1,0:T(8,128)S(1)}, f32[2,1024,256]{2,1,0:T(8,128)}, u32[]{:S(2)}) copy-start(f32[2,1024,256]{2,1,0:T(8,128)} %param.12) | copy-start | bytes 6291460
  61.3 1.7 copy-start.3
  244.6 3.8 copy-start.2
  248.1 286.3 %all-gather.7.cloned.1.call-start = ((), (), s32[]{:S(2)}) async-start(), calls=%async_computation.3 | async-start | bytes 17825792 | tf_op jit(solution)/shard_map/all_gather | solution.py:171
  437.3 4.1 copy-start.8
  441.4 175.4 %copy-start.9 = (s32[48]{0:T(128)}, s32[48]{0:T(128)S(1)}, u32[]{:S(2)}) copy-start(s32[48]{0:T(128)S(1)} %get-tuple-element.211) | copy-start | bytes 580
  660.1 0.7 copy-start.4
  665.2 4.0 copy-start.5
  665.2 4.0 copy-start.10
  670.3 16.0 %all-to-all-start.2 = ((f32[8,128,128]{2,1,0:T(8,128)}), f32[8,128,128]{2,1,0:T(8,128)}, u32[]{:S(2)}, u32[]{:S(2)}) async-start(f32[8,128,128]{2,1,0:T(8,128)} %broadcast_in_dim.147), calls=%async_computation.2 | async-start | bytes 1048576 | tf_op jit(solution)/shard_map/all_to_all | solution.py:30
  687.5 3.2 copy-start.6
Sparse Core Ops, SparseCore 0:
  248.2 110.0 all-gather.8
  440.8 93.4 all-gather.6
where the time goes:
time: 703 us; the launch traced here: 697 us
  local copies, waits for them, and re-layouts  171 us (24%)
  matrix products  154 us (22%)
  blocking collectives  95.2 us (14%)
  waiting for transfers between devices  93.4 us (13%)
  other arithmetic  77 us (11%)
  loops' own time  75.8 us (11%)
  starting transfers between devices  15.9 us (2%)
  between operations  15.3 us (2%)
    dot_general x40, matrix products, add_block(): jnp.einsum('tij,tjd->tid', weights_now, picked, precision=HIGHEST)  136 us
    all_gather x1, waiting for transfers between devices, on_device(): lax.all_gather(source_embed, COL, axis=0, tiled=True)  85.5 us
    gather x40, local copies, waits for them, and re-layouts, add_block(): picked = lookup[block_cols[:, block_index]]  81 us
    all_gather x12, blocking collectives, joined_all(): pieces = jax.tree.map(lambda part: lax.all_gather(part, axis), array)  77.7 us
    another operation x2, loops' own time, aggregate(): lax.scan(add_block, (start_sum, start_deg), jnp.arange(block_vals.shape[1]))  75.8 us
    reduce_sum x40, other arithmetic, add_block(): degree = degree + jnp.sum(weights_now, axis=2)  48.9 us
    dynamic_slice x40, local copies, waits for them, and re-layouts, aggregate(): lax.scan(add_block, (start_sum, start_deg), jnp.arange(block_vals.shape[1]))  23.6 us
    all_to_all x1, blocking collectives, from_everyone(): lax.all_to_all(jnp.broadcast_to(array[None], (size, *array.shape)), axis,...  17.5 us
  transfers between devices with their start and end apart: 4, of which 2 were waited for; matrix products, arithmetic and copies ran while one was open for 27% of the time, Pallas kernels for 0%

commit v1 on v0

--- a/solution.py
+++ b/solution.py
@@ -168,9 +168,9 @@
         -1, TILE, feat_width
     )
     target_tiles = target_group[cols_here]
-    source_group = lax.all_gather(source_embed, COL, axis=0, tiled=True).reshape(
-        -1, TILE, feat_width
-    )
+    source_group = jnp.concatenate(
+        lax.all_to_all(jnp.stack([source_embed] * lax.axis_size(COL)), COL, 0, 0), axis=0
+    ).reshape(-1, TILE, feat_width)
     source_tiles = source_group[rows_here]
     logits = (
         SHARPNESS

time: 703 us -> 734 us (1.044)
  waiting for transfers between devices: 93.4 us -> 117 us
  local copies, waits for them, and re-layouts: 171 us -> 179 us
    all_gather x1, waiting for transfers between devices: 0.02 us -> 109 us  [on_device(): lax.all_gather(target_embed, 'row', axis=0, tiled=True)]
    all_gather x1 -> x0, waiting for transfers between devices: 85.5 us -> none  [on_device(): lax.all_gather(source_embed, COL, axis=0, tiled=True)]
  transfers between devices with their start and end apart: 4 -> 4, of which waited for: 2 -> 2; matrix products, arithmetic and copies ran while one was open for 27% -> 26% of each run, Pallas kernels for 0% -> 0%
where the time goes in v1:
time: 734 us; the launch traced here: 728 us
  local copies, waits for them, and re-layouts  179 us (24%)
  matrix products  151 us (21%)
  waiting for transfers between devices  117 us (16%)
  blocking collectives  92.2 us (13%)
  other arithmetic  76.8 us (10%)
  loops' own time  75.8 us (10%)
  starting transfers between devices  22.1 us (3%)
  between operations  15.2 us (2%)
    dot_general x40, matrix products, add_block(): jnp.einsum('tij,tjd->tid', weights_now, picked, precision=HIGHEST)  134 us
    all_gather x1, waiting for transfers between devices, on_device(): lax.all_gather(target_embed, 'row', axis=0, tiled=True)  109 us
    gather x40, local copies, waits for them, and re-layouts, add_block(): picked = lookup[block_cols[:, block_index]]  80.9 us
    all_gather x12, blocking collectives, joined_all(): pieces = jax.tree.map(lambda part: lax.all_gather(part, axis), array)  78 us
    another operation x2, loops' own time, aggregate(): lax.scan(add_block, (start_sum, start_deg), jnp.arange(block_vals.shape[1]))  75.8 us
    reduce_sum x40, other arithmetic, add_block(): degree = degree + jnp.sum(weights_now, axis=2)  48.9 us
    dynamic_slice x40, local copies, waits for them, and re-layouts, aggregate(): lax.scan(add_block, (start_sum, start_deg), jnp.arange(block_vals.shape[1]))  23.5 us
  transfers between devices with their start and end apart: 4, of which 2 were waited for; matrix products, arithmetic and copies ran while one was open for 26% of the time, Pallas kernels for 0%

profile of v1, /device:TPU:1, one launch (start us, length us, event | category | flops | bytes accessed | tf_op | source)
XLA Modules:
  0.0 727.9 jit_solution(10188799398789061428)
XLA Ops:
  7.9 12.6 %gather_fusion.4 = f32[1024,256]{1,0:T(8,128)S(1)} fusion(f32[2,1024,256]{2,1,0:T(8,128)} %param.12, s32[1024]{0:T(1024)S(1)} %bitcast.240), kind=kCustom, calls=%fused_computation.4 | custom fusion | bytes 2105344 | tf_op jit(solution)/shard_map/vmap()/gather | solution.py:105
  22.4 11.5 %all-to-all-start = ((f32[2,512,256]{2,0,1:T(2,128)}), f32[2,512,256]{2,0,1:T(2,128)S(1)}, u32[]{:S(2)}, u32[]{:S(2)}) async-start(f32[2,512,256]{2,0,1:T(2,128)} %copy.24), calls=%async_computation | async-start | bytes 2097152 | tf_op jit(solution)/shard_map/all_to_all | solution.py:143
  33.9 12.9 %fusion.125 = (bf16[1,8,20,128,128]{4,3,2,1,0:T(8,128)(2,1)}, bf16[1,8,20,128,128]{4,3,2,1,0:T(8,128)(2,1)}) fusion(bf16[2,8,20,128,128]{4,3,2,1,0:T(8,128)(2,1)} %param.13), kind=kLoop, calls=%fused_computation.219 | loop fusion | bytes 20971520 | tf_op jit(solution)/shard_map/slice | solution.py:152
  48.6 12.8 %copy_bitcast_fusion = (bf16[8,20,128,128]{3,2,0,1:T(8,128)(2,1)}, bf16[8,20,128,128]{3,2,0,1:T(8,128)(2,1)}) fusion(bf16[1,8,20,128,128]{4,3,2,1,0:T(8,128)(2,1)} %get-tuple-element.195, bf16[1,8,20,128,128]{4,3,2,1,0:T(8,128)(2,1)} %get-tuple-element.196), kind=kLoop, calls=%fused_computation.33 | loop fusion | bytes 20971520 | tf_op jit(solution)/shard_map/squeeze | solution.py:152
  64.3 180.5 %while.26 = (s32[]{:T(128)}, f32[8,128,256]{2,1,0:T(8,128)}, f32[8,128]{1,0:T(8,128)S(1)}, s32[20]{0:T(128)S(1)}, bf16[8,20,128,128]{3,2,0,1:T(8,128)(2,1)}, /*i...) while((s32[]{:T(128)}, f32[8,128,256]{2,1,0:T(8,128)}, ...), condition=%wide.region_2.3_spmd.clone, body=%wide.region_0.2_spmd.clone.sunk | while | flops 403834912 | bytes 5788086 | solution.py:97
  68.7 3.0 convolution_add_fusion.4
  77.4 3.4 convolution_add_fusion.4
  86.5 3.4 convolution_add_fusion.4
  95.5 3.4 convolution_add_fusion.4
  104.6 3.4 convolution_add_fusion.4
  113.6 3.4 convolution_add_fusion.4
  122.6 3.4 convolution_add_fusion.4
  131.7 3.4 convolution_add_fusion.4
  140.7 3.4 convolution_add_fusion.4
  149.8 3.4 convolution_add_fusion.4
  158.8 3.4 convolution_add_fusion.4
  167.9 3.4 convolution_add_fusion.4
  176.9 3.4 convolution_add_fusion.4
  186.0 3.4 convolution_add_fusion.4
  195.0 3.4 convolution_add_fusion.4
  204.0 3.4 convolution_add_fusion.4
  213.1 3.4 convolution_add_fusion.4
  222.1 3.4 convolution_add_fusion.4
  231.2 3.4 convolution_add_fusion.4
  240.2 3.4 convolution_add_fusion.4
  247.3 7.3 %stack.2 = f32[16,1024,256]{2,1,0:T(8,128)} broadcast(f32[1024,256]{1,0:T(8,128)S(1)} %fusion.18), dimensions={1,2} | broadcast | bytes 17825792 | tf_op jit(solution)/shard_map/stack | solution.py:172
  254.7 6.2 all-to-all-start.1
  263.5 184.0 %while.27 = (s32[]{:T(128)}, f32[8,128,256]{2,1,0:T(8,128)}, f32[8,128]{1,0:T(8,128)S(1)}, s32[20]{0:T(128)S(1)}, bf16[8,20,128,128]{3,2,0,1:T(8,128)(2,1)}, /*i...) while((s32[]{:T(128)}, f32[8,128,256]{2,1,0:T(8,128)}, ...), condition=%wide.region_5.6_spmd.clone, body=%wide.region_3.5_spmd.clone.sunk | while | flops 403834912 | bytes 5788086 | solution.py:97
  276.9 3.3 convolution_add_fusion.5
  286.2 3.3 convolution_add_fusion.5
  295.4 3.3 convolution_add_fusion.5
  304.6 3.3 convolution_add_fusion.5
  313.8 3.3 convolution_add_fusion.5
  323.0 3.3 convolution_add_fusion.5
  332.3 3.3 convolution_add_fusion.5
  341.5 3.3 convolution_add_fusion.5
  350.7 3.3 convolution_add_fusion.5
  359.9 3.3 convolution_add_fusion.5
  369.1 3.3 convolution_add_fusion.5
  378.4 3.3 convolution_add_fusion.5
  387.6 3.3 convolution_add_fusion.5
  396.8 3.3 convolution_add_fusion.5
  406.0 3.3 convolution_add_fusion.5
  415.2 3.3 convolution_add_fusion.5
  424.5 3.3 convolution_add_fusion.5
  433.7 3.3 convolution_add_fusion.5
  442.9 3.3 convolution_add_fusion.5
  452.0 108.7 %all-gather.6.cloned.1.call-done = f32[8192,256]{1,0:T(8,128)} async-done(((f32[1024,256]{1,0:T(8,128)}), f32[8192,256]{1,0:T(8,128)}) %all-gather.6.cloned.1.call-update) | async-done | bytes 8388624 | tf_op jit(solution)/shard_map/all_gather | solution.py:167
  560.8 7.0 gather_fusion.3
  567.8 9.4 %gather_fusion.2 = f32[48,128,256]{2,1,0:T(8,128)} fusion(f32[128,128,256]{2,1,0:T(8,128)} %bitcast.11, s32[1024]{0:T(1024)S(1)} %get-tuple-element.226), kind=kCustom, calls=%fused_computation.2 | custom fusion | bytes 12583104 | tf_op jit(solution)/shard_map/gather | solution.py:174
  577.2 9.2 %fusion.14 = (f32[48,128]{1,0:T(8,128)S(1)}, f32[48,128,128]{2,1,0:T(8,128)S(1)}) fusion(f32[48,128]{1,0:T(8,128)S(1)} %fusion.88, pred[48]{0:T(512)(128)(4,1)S(1)} %iota_compare_fusion.13, f32[48,128,256]{2,1,0:T(8,128)} %gather_fusion.2, f32[48,128,256]{2,1,0:T(8,128)} %gather_fusion.3), kind=kOutput, calls=%fused_computation.46 | convolution fusion | flops 2419058688 | bytes 15777840 | tf_op jit(solution)/shard_map/sid,sjd->sij/dot_general | solution.py:178
  587.8 3.8 all-gather
  594.1 3.8 all-gather.1
  597.9 9.7 %all_gather.62 = f32[4,128,128]{2,1,0:T(8,128)S(1)} all-gather(f32[1,128,128]{2,1,0:T(8,128)S(1)} %get-tuple-element.194), channel_id=1, replica_groups=mesh['row'=8,'col_0'=2,'col_1'=4,'col_2'=2] {'col_1'}, dimensions={0}, use_global_device_ids=true | all-gather | bytes 327680 | tf_op jit(solution)/shard_map/all_gather | solution.py:21
  607.6 9.4 %all_gather.66 = f32[4,128,128]{2,1,0:T(8,128)S(1)} all-gather(f32[1,128,128]{2,1,0:T(8,128)S(1)} %get-tuple-element.193), channel_id=1, replica_groups=mesh['row'=8,'col_0'=2,'col_1'=4,'col_2'=2] {'col_1'}, dimensions={0}, use_global_device_ids=true | all-gather | bytes 327680 | tf_op jit(solution)/shard_map/all_gather | solution.py:21
  617.0 10.7 %all_gather.63 = f32[2,128,128]{2,1,0:T(8,128)S(1)} all-gather(f32[1,128,128]{2,1,0:T(8,128)S(1)} %get-tuple-element.192), channel_id=1, replica_groups=mesh['row'=8,'col_0'=2,'col_1'=4,'col_2'=2] {'col_2'}, dimensions={0}, use_global_device_ids=true | all-gather | bytes 196608 | tf_op jit(solution)/shard_map/all_gather | solution.py:21
  633.4 14.2 %all_to_all.20 = f32[8,128,128]{2,1,0:T(8,128)S(1)} all-to-all(f32[8,128,128]{2,1,0:T(8,128)S(1)} %broadcast_in_dim.144), channel_id=1, replica_groups=mesh['row'=8,'col_0'=2,'col_1'=4,'col_2'=2] {'row'}, dimensions={0} | all-to-all | bytes 1048576 | tf_op jit(solution)/shard_map/all_to_all | solution.py:30
  650.6 3.8 all-gather.2
  656.9 3.8 all-gather.3
  660.7 9.4 %all_gather.70 = f32[4,128,128]{2,1,0:T(8,128)S(1)} all-gather(f32[1,128,128]{2,1,0:T(8,128)S(1)} %get-tuple-element.186), channel_id=1, replica_groups=mesh['row'=8,'col_0'=2,'col_1'=4,'col_2'=2] {'col_1'}, dimensions={0}, use_global_device_ids=true | all-gather | bytes 327680 | tf_op jit(solution)/shard_map/all_gather | solution.py:21
  670.1 9.4 %all_gather.74 = f32[4,128,128]{2,1,0:T(8,128)S(1)} all-gather(f32[1,128,128]{2,1,0:T(8,128)S(1)} %get-tuple-element.185), channel_id=1, replica_groups=mesh['row'=8,'col_0'=2,'col_1'=4,'col_2'=2] {'col_1'}, dimensions={0}, use_global_device_ids=true | all-gather | bytes 327680 | tf_op jit(solution)/shard_map/all_gather | solution.py:21
  680.1 10.4 %all_gather.71 = f32[2,128,128]{2,1,0:T(8,128)S(1)} all-gather(f32[1,128,128]{2,1,0:T(8,128)S(1)} %get-tuple-element.184), channel_id=1, replica_groups=mesh['row'=8,'col_0'=2,'col_1'=4,'col_2'=2] {'col_2'}, dimensions={0}, use_global_device_ids=true | all-gather | bytes 196608 | tf_op jit(solution)/shard_map/all_gather | solution.py:21
  700.8 4.1 all-to-all-start.3
  708.8 7.9 %all-to-all-done.3 = f32[8,128,128]{2,1,0:T(8,128)} async-done(((f32[8,128,128]{2,1,0:T(8,128)}), f32[8,128,128]{2,1,0:T(8,128)}, u32[]{:S(2)}, u32[]{:S(2)}) %all-to-all-start.3) | async-done | bytes 524320 | tf_op jit(solution)/shard_map/all_to_all | solution.py:30
  (388 shorter events, 207.9 us)
Async XLA Ops:
  7.2 239.1 %copy-start = (f32[256,256]{1,0:T(8,128)S(1)}, f32[256,256]{1,0:T(8,128)}, u32[]{:S(2)}) copy-start(f32[256,256]{1,0:T(8,128)} %param.17) | copy-start | bytes 786436
  22.4 39.0 %all-to-all-start = ((f32[2,512,256]{2,0,1:T(2,128)}), f32[2,512,256]{2,0,1:T(2,128)S(1)}, u32[]{:S(2)}, u32[]{:S(2)}) async-start(f32[2,512,256]{2,0,1:T(2,128)} %copy.24), calls=%async_computation | async-start | bytes 2097152 | tf_op jit(solution)/shard_map/all_to_all | solution.py:143
  33.9 13.0 %copy-start.11 = (s32[2,8]{1,0:T(2,128)S(1)}, s32[2,8]{1,0:T(2,128)}, u32[]{:S(2)}) copy-start(s32[2,8]{1,0:T(2,128)} %param.15) | copy-start | bytes 196
  33.9 13.0 %copy-start.7 = (s32[2,8,20]{2,1,0:T(8,128)S(1)}, s32[2,8,20]{2,1,0:T(8,128)}, u32[]{:S(2)}) copy-start(s32[2,8,20]{2,1,0:T(8,128)} %param.14) | copy-start | bytes 3844
  33.9 13.2 %copy-start.1 = (f32[2,1024,256]{2,1,0:T(8,128)S(1)}, f32[2,1024,256]{2,1,0:T(8,128)}, u32[]{:S(2)}) copy-start(f32[2,1024,256]{2,1,0:T(8,128)} %param.12) | copy-start | bytes 6291460
  61.4 1.7 copy-start.3
  254.7 6.5 copy-start.2
  254.7 313.1 %all-to-all-start.1 = ((f32[16,1024,256]{2,1,0:T(8,128)}), f32[16,1024,256]{2,1,0:T(8,128)}, u32[]{:S(2)}, u32[]{:S(2)}) async-start(f32[16,1024,256]{2,1,0:T(8,128)} %stack.2), calls=%async_computation.1 | async-start | bytes 33554432 | tf_op jit(solution)/shard_map/all_to_all | solution.py:172
  260.9 299.9 %all-gather.6.cloned.1.call-start = ((), (), s32[]{:S(2)}) async-start(), calls=%async_computation.4 | async-start | bytes 9437184 | tf_op jit(solution)/shard_map/all_gather | solution.py:167
  447.5 4.1 copy-start.8
  451.7 196.1 %copy-start.9 = (s32[48]{0:T(128)}, s32[48]{0:T(128)S(1)}, u32[]{:S(2)}) copy-start(s32[48]{0:T(128)S(1)} %get-tuple-element.211) | copy-start | bytes 580
  690.5 0.7 copy-start.4
  695.7 4.0 copy-start.5
  695.7 4.0 copy-start.10
  700.8 15.9 %all-to-all-start.3 = ((f32[8,128,128]{2,1,0:T(8,128)}), f32[8,128,128]{2,1,0:T(8,128)}, u32[]{:S(2)}, u32[]{:S(2)}) async-start(f32[8,128,128]{2,1,0:T(8,128)} %broadcast_in_dim.147), calls=%async_computation.3 | async-start | bytes 1048576 | tf_op jit(solution)/shard_map/all_to_all | solution.py:30
  717.9 3.2 copy-start.6
Sparse Core Ops, SparseCore 0:
  451.1 109.6 all-gather.5
